TPU v7x, 32 devices: a whole 2x2x4 slice. The times are simulated.
32 devices in a mesh: row: 4 (over y, x), col: 8 (over z, core).
Axes of the slice: x: 2, y: 2, z: 4, core: 2. Of those that a mesh axis runs over, the one named last changes fastest.
Arguments:
- stiffness: float32 [12, 4, 128, 6144], P(None, 'row', None, 'col'), may hold values from -8 to 8
- lower_first: float32 [1024, 10, 4, 128], P('col', None, 'row'), may hold values from -0.1875 to 0.1875
- lower_second: float32 [1024, 8, 4, 128], P('col', None, 'row'), may hold values from -0.1875 to 0.1875
- diag_inv: float32 [2, 1024, 2, 4, 128], P(None, 'col', None, 'row'), as said below
Outputs:
- reduced: float32 [12, 4, 128, 6144], P(None, 'row', None, 'col')
Inputs may be any that keep to these rules, and one draw needn't show every extreme that they name: Each block of diag_inv, read as a 1024 x 1024 matrix, is zero above its diagonal and has a positive diagonal.
All inputs are finite; a program needn't handle non-finite values.
Results may differ from a plain program's by a relative error of at most 0.000086.
Values sent between devices are 32-bit elements; how exact they have to be, the bound alone decides.
A program may use at most 128 MiB of HBM per device.

v0:
```python
import jax
import jax.numpy as jnp
from jax import lax
from jax.sharding import PartitionSpec as P


def product(left, right):
    return jnp.dot(left, right, precision=lax.Precision.HIGHEST, preferred_element_type=jnp.float32)


def apply_cols(columns, factor):
    return lax.dot_general(
        columns,
        factor,
        (((0,), (0,)), ((), ())),
        precision=lax.Precision.HIGHEST,
        preferred_element_type=jnp.float32,
    )


def shards(stiffness, lower_first, lower_second, diag_inv):
    cycles = stiffness.shape[0]
    rblk = stiffness.shape[2]
    cdev = stiffness.shape[3]
    pcount = diag_inv.shape[2]
    nrow = lax.axis_size("row")
    nb = diag_inv.shape[1] * lax.axis_size("col")
    height = pcount * rblk
    matrix_rows = stiffness.reshape(cycles * rblk, cdev)
    inv_cols = lax.all_gather(diag_inv, "col", axis=1, tiled=True)
    inverse = inv_cols.reshape(2, nb, height)

    def own_rows(solved):
        grouped = solved.reshape(pcount, nrow, rblk, cdev)
        mine = lax.dynamic_slice_in_dim(grouped, lax.axis_index("row"), 1, 1)
        return mine.reshape(height, cdev)

    w_first = lax.psum(product(inverse[0], matrix_rows[:height]), "row")
    coupling = lax.all_gather(lower_first[:, :pcount], "col", axis=0, tiled=True).reshape(
        nb, height
    )
    w_second = lax.psum(
        product(inverse[1], matrix_rows[height : 2 * height] - apply_cols(coupling, w_first)), "row"
    )
    pieces = (
        lax.all_gather(lower_first[:, pcount:], "col", axis=0, tiled=True),
        lax.all_gather(lower_second, "col", axis=0, tiled=True),
    )
    count = pieces[0].shape[0]
    first_piece = pieces[0].reshape(count, -1)
    second_piece = pieces[1].reshape(count, -1)
    remain = (
        matrix_rows[2 * height :]
        - apply_cols(first_piece, w_first)
        - apply_cols(second_piece, w_second)
    )
    stacked = jnp.concatenate([own_rows(w_first), own_rows(w_second), remain], axis=0)
    return stacked.reshape(cycles, 1, rblk, cdev)


def solution(mesh):
    placed = (
        P(None, "row", None, "col"),
        P("col", None, "row", None),
        P("col", None, "row", None),
        P(None, "col", None, "row", None),
    )
    return jax.shard_map(
        shards, mesh=mesh, in_specs=placed, out_specs=P(None, "row", None, "col"), check_vma=False
    )
```

profile of v0, /device:TPU:0, one launch (start us, length us, event | category | flops | bytes accessed | tf_op | source)
XLA Modules:
  0.0 378.0 jit_solution(10535140194078627687)
XLA Ops:
  7.3 1.6 slice.37
  8.9 1.5 fusion.16
  10.4 30.4 %all-gather.5.cloned.1.call-done = f32[2,1024,2,1,128]{4,3,2,1,0:T(1,128)} async-done(((f32[2,128,2,1,128]{4,3,2,1,0:T(1,128)}), f32[2,1024,2,1,128]{4,3,2,1,0:T(1,128)}) %all-gather.5.cloned.1.call-update) | async-done | bytes 2097168 | tf_op jit(solution)/shard_map/all_gather | solution.py:30
  40.8 7.8 %slice_reduce_fusion = (f32[1024,2,128]{2,1,0:T(2,128)S(1)}, f32[1024,2,128]{2,1,0:T(2,128)S(1)}) fusion(f32[2,1024,2,1,128]{4,3,2,1,0:T(1,128)} %all-gather.5.cloned.1.call-done), kind=kLoop, calls=%fused_computation.19 | loop fusion | bytes 4194304 | tf_op jit(solution)/shard_map/slice | solution.py:43
  48.7 4.4 %fusion.13 = f32[1024,768]{1,0:T(8,128)} fusion(f32[256,768]{1,0:T(8,128)S(1)} %bitcast.71, f32[128,8,2,128]{3,2,1,0:T(2,128)S(1)} %bitcast.68), kind=kOutput, calls=%fused_computation.16 | convolution fusion | flops 2415919104 | bytes 4980736 | tf_op jit(solution)/shard_map/dot_general | solution.py:8
  53.6 10.5 %all-gather.7.cloned.1.call-done = f32[1024,2,1,128]{3,1,2,0:T(2,128)} async-done(((f32[128,2,1,128]{3,1,2,0:T(2,128)}), f32[1024,2,1,128]{3,1,2,0:T(2,128)}) %all-gather.7.cloned.1.call-update) | async-done | bytes 1048592 | tf_op jit(solution)/shard_map/all_gather | solution.py:39
  64.1 89.7 %all-reduce.3.cloned.1.call-done = f32[1024,768]{1,0:T(8,128)} async-done(((f32[1024,768]{1,0:T(8,128)}), f32[1024,768]{1,0:T(8,128)}) %all-reduce.3.cloned.1.call-update) | async-done | bytes 3145744 | tf_op jit(solution)/shard_map/psum | solution.py:38
  153.8 7.2 %fusion.8 = f32[256,768]{0,1:T(8,128)S(1)} fusion(f32[256,768]{0,1:T(8,128)S(1)} %copy.21, f32[1024,768]{1,0:T(8,128)} %all-reduce.3.cloned.1.call-done, f32[128,8,2,128]{3,2,1,0:T(2,128)} %bitcast.76), kind=kOutput, calls=%fused_computation.11 | convolution fusion | flops 2416115712 | bytes 5767168 | tf_op jit(solution)/shard_map/dot_general | solution.py:12
  161.0 4.4 %convolution_bitcast_fusion = f32[1024,768]{0,1:T(8,128)} fusion(f32[256,768]{0,1:T(8,128)S(1)} %fusion.8, f32[128,8,2,128]{3,2,1,0:T(2,128)S(1)} %bitcast.67), kind=kOutput, calls=%fused_computation.9 | convolution fusion | flops 2415919104 | bytes 4980736 | tf_op jit(solution)/shard_map/dot_general | solution.py:8
  166.3 0.8 slice.41
  167.2 3.8 slice.39
  170.9 4.1 %copy.22 = f32[1024,768]{0,1:T(8,128)} copy(f32[1024,768]{1,0:T(8,128)} %bitcast.65) | data formatting | bytes 6291456 | tf_op jit(solution)/shard_map/slice | solution.py:53
  175.1 0.9 constant_dynamic-slice_fusion
  176.0 2.3 copy.20
  178.3 74.2 %all-reduce.5.cloned.1.call-done = f32[1024,768]{0,1:T(8,128)} async-done(((f32[1024,768]{0,1:T(8,128)}), f32[1024,768]{0,1:T(8,128)}) %all-reduce.5.cloned.1.call-update) | async-done | bytes 3145744 | tf_op jit(solution)/shard_map/psum | solution.py:42
  252.5 5.1 %reshape.36 = f32[2,4,128,768]{2,1,0,3:T(4,128)} reshape(f32[1024,768]{0,1:T(8,128)} %all-reduce.5.cloned.1.call-done) | data formatting | bytes 6291456 | tf_op jit(solution)/shard_map/reshape | solution.py:34
  257.7 4.6 %dynamic-slice_reduce_fusion = f32[2,128,768]{1,0,2:T(2,128)S(1)} fusion(f32[2,4,128,768]{2,1,0,3:T(4,128)} %reshape.36, s32[]{:T(128)S(6)} %select_n.4), kind=kLoop, calls=%fused_computation.22 | loop fusion | bytes 1572868 | tf_op jit(solution)/shard_map/dynamic_slice | solution.py:35
  262.2 0.9 copy.54
  263.2 37.7 %all-gather.11.cloned.1.call-done = f32[1024,8,1,128]{3,1,2,0:T(8,128)} async-done(((f32[128,8,1,128]{3,1,2,0:T(8,128)}), f32[1024,8,1,128]{3,1,2,0:T(8,128)}) %all-gather.11.cloned.1.call-update) | async-done | bytes 4194320 | tf_op jit(solution)/shard_map/all_gather | solution.py:47
  300.9 14.8 %fusion = f32[768,1024]{1,0:T(8,128)} fusion(f32[1024,768]{0,1:T(8,128)} %all-reduce.5.cloned.1.call-done, f32[128,8,8,128]{3,2,1,0:T(8,128)} %bitcast.66), kind=kOutput, calls=%fused_computation.1 | convolution fusion | flops 9663676416 | bytes 10485760 | tf_op jit(solution)/shard_map/dot_general | solution.py:12
  315.6 32.4 %all-gather.9.cloned.1.call-done = f32[1024,8,1,128]{3,1,2,0:T(8,128)} async-done(((f32[128,8,1,128]{3,1,2,0:T(8,128)}), f32[1024,8,1,128]{3,1,2,0:T(8,128)}) %all-gather.9.cloned.1.call-update) | async-done | bytes 4194320 | tf_op jit(solution)/shard_map/all_gather | solution.py:46
  348.0 14.4 %bitcast_subtract_fusion = f32[1024,768]{0,1:T(8,128)S(1)} fusion(f32[768,1024]{1,0:T(8,128)} %fusion, f32[1024,768]{0,1:T(8,128)} %copy.22, f32[1024,768]{1,0:T(8,128)S(1)} %copy-done, f32[128,8,8,128]{3,2,1,0:T(8,128)} %bitcast.69), kind=kOutput, calls=%fused_computation.7 | convolution fusion | flops 9665249280 | bytes 16777216 | tf_op jit(solution)/shard_map/dot_general | solution.py:12
  362.5 2.6 pad_maximum_fusion
  365.1 6.0 %copy.18 = f32[1536,768]{1,0:T(8,128)} copy(f32[1536,768]{0,1:T(8,128)} %pad_maximum_fusion) | data formatting | bytes 9437184 | tf_op jit(solution)/shard_map/concatenate | solution.py:57
  (21 shorter events, 2.2 us)
Async XLA Ops:
  6.5 34.3 %all-gather.5.cloned.1.call-start = ((), (), s32[]{:S(2)}) async-start(), calls=%async_computation | async-start | bytes 2359296 | tf_op jit(solution)/shard_map/all_gather | solution.py:30
  7.3 56.9 %all-gather.7.cloned.1.call-start = ((), (), s32[]{:S(2)}) async-start(), calls=%async_computation.2 | async-start | bytes 1179648 | tf_op jit(solution)/shard_map/all_gather | solution.py:39
  8.9 144.9 %all-reduce.3.cloned.1.call-start = ((), (), s32[]{:S(2)}) async-start(), calls=%async_computation.1 | async-start | bytes 6291456 | tf_op jit(solution)/shard_map/psum | solution.py:38
  53.1 199.4 %all-reduce.5.cloned.1.call-start = ((), (), s32[]{:S(2)}) async-start(), calls=%async_computation.3 | async-start | bytes 6291456 | tf_op jit(solution)/shard_map/psum | solution.py:42
  161.0 5.3 %copy-start.3 = (f32[128,10,1,128]{3,2,1,0:T(1,128)S(1)}, f32[128,10,1,128]{3,2,1,0:T(1,128)}, u32[]{:S(2)}) copy-start(f32[128,10,1,128]{3,2,1,0:T(1,128)} %param.5) | copy-start | bytes 1966084
  165.4 135.4 %all-gather.11.cloned.1.call-start = ((), (), s32[]{:S(2)}) async-start(), calls=%async_computation.5 | async-start | bytes 4718592 | tf_op jit(solution)/shard_map/all_gather | solution.py:47
  166.0 182.0 %all-gather.9.cloned.1.call-start = ((), (), s32[]{:S(2)}) async-start(), calls=%async_computation.4 | async-start | bytes 4718592 | tf_op jit(solution)/shard_map/all_gather | solution.py:46
  170.9 4.1 %copy-start = (f32[1024,768]{1,0:T(8,128)S(1)}, f32[1024,768]{1,0:T(8,128)}, u32[]{:S(2)}) copy-start(f32[1024,768]{1,0:T(8,128)} %all-reduce.3.cloned.1.call-done) | copy-start | bytes 9437188
  348.0 14.4 %copy-start.1 = (f32[256,768]{0,1:T(8,128)S(1)}, f32[256,768]{0,1:T(8,128)}, u32[]{:S(2)}) copy-start(f32[256,768]{0,1:T(8,128)} %copy.20) | copy-start | bytes 2359300
  348.0 14.4 %copy-start.2 = (f32[96,8,2,128]{3,1,2,0:T(8,128)S(1)}, f32[96,8,2,128]{3,1,2,0:T(8,128)}, u32[]{:S(2)}) copy-start(f32[96,8,2,128]{3,1,2,0:T(8,128)} %copy.54) | copy-start | bytes 2359300
Sparse Core Ops, SparseCore 0:
  8.9 31.8 all-gather.4
  42.4 21.6 all-gather.6
  67.2 86.5 all-reduce.2
  165.5 86.9 all-reduce.4
  254.0 46.8 all-gather.10
  302.3 45.6 all-gather.8
where the time goes:
time: 378 us
  waiting for transfers between devices  276 us (73%)
  matrix products  45.1 us (12%)
  local copies, waits for them, and re-layouts  39.8 us (11%)
  between operations  13.6 us (4%)
    psum x1, waiting for transfers between devices, shards(): w_first = lax.psum(product(inverse[0], matrix_rows[:height]), 'row')  89.7 us
    psum x1, waiting for transfers between devices, shards(): lax.psum(product(inverse[1], matrix_rows[height:2 * height] - apply_cols(...  74.2 us
    all_gather x1, waiting for transfers between devices, shards(): lax.all_gather(lower_second, 'col', axis=0, tiled=True)  37.7 us
    dot_general x3, matrix products, apply_cols(): lax.dot_general(columns, factor, (((0,), (0,)), ((), ())), precision=lax....  36.4 us
    all_gather x1, waiting for transfers between devices, shards(): lax.all_gather(lower_first[:, pcount:], 'col', axis=0, tiled=True)  32.4 us
    all_gather x1, waiting for transfers between devices, shards(): inv_cols = lax.all_gather(diag_inv, 'col', axis=1, tiled=True)  30.4 us
    all_gather x1, waiting for transfers between devices, shards(): lax.all_gather(lower_first[:, :pcount], 'col', axis=0, tiled=True)  10.5 us
    dot_general x2, matrix products, product(): jnp.dot(left, right, precision=lax.Precision.HIGHEST, preferred_element_t...  8.73 us
  transfers between devices with their start and end apart: 6, of which 6 were waited for; matrix products, arithmetic and copies ran while one was open for 14% of the time, Pallas kernels for 0%

commit v1 on v0

--- a/solution.py
+++ b/solution.py
@@ -5,7 +5,7 @@
 
 
 def product(left, right):
-    return jnp.dot(left, right, precision=lax.Precision.HIGHEST, preferred_element_type=jnp.float32)
+    return jnp.dot(left, right, precision=lax.Precision.HIGH, preferred_element_type=jnp.float32)
 
 
 def apply_cols(columns, factor):
@@ -13,7 +13,7 @@
         columns,
         factor,
         (((0,), (0,)), ((), ())),
-        precision=lax.Precision.HIGHEST,
+        precision=lax.Precision.HIGH,
         preferred_element_type=jnp.float32,
     )
 

time: 378 us -> 370 us (0.979)
  matrix products: 45.1 us -> 30 us
  waiting for transfers between devices: 276 us -> 283 us
    dot_general x3, matrix products: 36.4 us -> 23.8 us  [apply_cols(): lax.dot_general(columns, factor, (((0,), (0,)), ((), ())), precision=lax....]
    all_gather x1, waiting for transfers between devices: 32.4 us -> 37.6 us  [shards(): lax.all_gather(lower_first[:, pcount:], 'col', axis=0, tiled=True)]
  transfers between devices with their start and end apart: 6 -> 6, of which waited for: 6 -> 6; matrix products, arithmetic and copies ran while one was open for 14% -> 13% of each run, Pallas kernels for 0% -> 0%
where the time goes in v1:
time: 370 us; the launch traced here: 369 us
  waiting for transfers between devices  283 us (76%)
  local copies, waits for them, and re-layouts  39.8 us (11%)
  matrix products  30 us (8%)
  between operations  13.6 us (4%)
    psum x1, waiting for transfers between devices, shards(): w_first = lax.psum(product(inverse[0], matrix_rows[:height]), 'row')  89.7 us
    psum x1, waiting for transfers between devices, shards(): lax.psum(product(inverse[1], matrix_rows[height:2 * height] - apply_cols(...  74.3 us
    all_gather x1, waiting for transfers between devices, shards(): lax.all_gather(lower_second, 'col', axis=0, tiled=True)  37.7 us
    all_gather x1, waiting for transfers between devices, shards(): lax.all_gather(lower_first[:, pcount:], 'col', axis=0, tiled=True)  37.6 us
    all_gather x1, waiting for transfers between devices, shards(): inv_cols = lax.all_gather(diag_inv, 'col', axis=1, tiled=True)  30.4 us
    dot_general x3, matrix products, apply_cols(): lax.dot_general(columns, factor, (((0,), (0,)), ((), ())), precision=lax....  23.8 us
    all_gather x1, waiting for transfers between devices, shards(): lax.all_gather(lower_first[:, :pcount], 'col', axis=0, tiled=True)  12 us
    slice x2, local copies, waits for them, and re-layouts, shards(): matrix_rows[2 * height:] - apply_cols(first_piece, w_first)  7.89 us
  transfers between devices with their start and end apart: 6, of which 6 were waited for; matrix products, arithmetic and copies ran while one was open for 13% of the time, Pallas kernels for 0%

profile of v1, /device:TPU:0, one launch (start us, length us, event | category | flops | bytes accessed | tf_op | source)
XLA Modules:
  0.0 369.2 jit_solution(9611690720741950493)
XLA Ops:
  7.3 1.6 slice.37
  8.9 1.5 fusion.16
  10.4 30.4 %all-gather.5.cloned.1.call-done = f32[2,1024,2,1,128]{4,3,2,1,0:T(1,128)} async-done(((f32[2,128,2,1,128]{4,3,2,1,0:T(1,128)}), f32[2,1024,2,1,128]{4,3,2,1,0:T(1,128)}) %all-gather.5.cloned.1.call-update) | async-done | bytes 2097168 | tf_op jit(solution)/shard_map/all_gather | solution.py:30
  40.8 7.8 %slice_reduce_fusion = (f32[1024,2,128]{2,1,0:T(2,128)S(1)}, f32[1024,2,128]{2,1,0:T(2,128)S(1)}) fusion(f32[2,1024,2,1,128]{4,3,2,1,0:T(1,128)} %all-gather.5.cloned.1.call-done), kind=kLoop, calls=%fused_computation.19 | loop fusion | bytes 4194304 | tf_op jit(solution)/shard_map/slice | solution.py:43
  48.7 3.1 fusion.13
  52.2 12.0 %all-gather.7.cloned.1.call-done = f32[1024,2,1,128]{3,1,2,0:T(2,128)} async-done(((f32[128,2,1,128]{3,1,2,0:T(2,128)}), f32[1024,2,1,128]{3,1,2,0:T(2,128)}) %all-gather.7.cloned.1.call-update) | async-done | bytes 1048592 | tf_op jit(solution)/shard_map/all_gather | solution.py:39
  64.1 89.7 %all-reduce.3.cloned.1.call-done = f32[1024,768]{1,0:T(8,128)} async-done(((f32[1024,768]{1,0:T(8,128)}), f32[1024,768]{1,0:T(8,128)}) %all-reduce.3.cloned.1.call-update) | async-done | bytes 3145744 | tf_op jit(solution)/shard_map/psum | solution.py:38
  153.8 4.8 %fusion.8 = f32[256,768]{0,1:T(8,128)S(1)} fusion(f32[256,768]{0,1:T(8,128)S(1)} %copy.21, f32[1024,768]{1,0:T(8,128)} %all-reduce.3.cloned.1.call-done, f32[128,8,2,128]{3,2,1,0:T(2,128)} %bitcast.76), kind=kOutput, calls=%fused_computation.11 | convolution fusion | flops 1208156160 | bytes 5767168 | tf_op jit(solution)/shard_map/dot_general | solution.py:12
  158.6 3.1 convolution_bitcast_fusion
  162.6 0.8 slice.41
  163.4 3.8 %slice.39 = f32[8,1,128,768]{3,2,1,0:T(8,128)} slice(f32[12,1,128,768]{3,2,1,0:T(8,128)} %param.4), slice={[4:12], [0:1], [0:128], [0:768]} | slice | bytes 6291456 | tf_op jit(solution)/shard_map/slice | solution.py:53
  167.2 4.1 %copy.22 = f32[1024,768]{0,1:T(8,128)} copy(f32[1024,768]{1,0:T(8,128)} %bitcast.65) | data formatting | bytes 6291456 | tf_op jit(solution)/shard_map/slice | solution.py:53
  171.3 0.9 constant_dynamic-slice_fusion
  172.3 2.3 copy.20
  174.6 74.3 %all-reduce.5.cloned.1.call-done = f32[1024,768]{0,1:T(8,128)} async-done(((f32[1024,768]{0,1:T(8,128)}), f32[1024,768]{0,1:T(8,128)}) %all-reduce.5.cloned.1.call-update) | async-done | bytes 3145744 | tf_op jit(solution)/shard_map/psum | solution.py:42
  248.8 5.1 %reshape.36 = f32[2,4,128,768]{2,1,0,3:T(4,128)} reshape(f32[1024,768]{0,1:T(8,128)} %all-reduce.5.cloned.1.call-done) | data formatting | bytes 6291456 | tf_op jit(solution)/shard_map/reshape | solution.py:34
  254.0 4.6 %dynamic-slice_reduce_fusion = f32[2,128,768]{1,0,2:T(2,128)S(1)} fusion(f32[2,4,128,768]{2,1,0,3:T(4,128)} %reshape.36, s32[]{:T(128)S(6)} %select_n.4), kind=kLoop, calls=%fused_computation.22 | loop fusion | bytes 1572868 | tf_op jit(solution)/shard_map/dynamic_slice | solution.py:35
  258.5 0.9 copy.54
  259.5 37.7 %all-gather.11.cloned.1.call-done = f32[1024,8,1,128]{3,1,2,0:T(8,128)} async-done(((f32[128,8,1,128]{3,1,2,0:T(8,128)}), f32[1024,8,1,128]{3,1,2,0:T(8,128)}) %all-gather.11.cloned.1.call-update) | async-done | bytes 4194320 | tf_op jit(solution)/shard_map/all_gather | solution.py:47
  297.2 9.6 %fusion = f32[768,1024]{1,0:T(8,128)} fusion(f32[1024,768]{0,1:T(8,128)} %all-reduce.5.cloned.1.call-done, f32[128,8,8,128]{3,2,1,0:T(8,128)} %bitcast.66), kind=kOutput, calls=%fused_computation.1 | convolution fusion | flops 4831838208 | bytes 10485760 | tf_op jit(solution)/shard_map/dot_general | solution.py:12
  306.8 37.6 %all-gather.9.cloned.1.call-done = f32[1024,8,1,128]{3,1,2,0:T(8,128)} async-done(((f32[128,8,1,128]{3,1,2,0:T(8,128)}), f32[1024,8,1,128]{3,1,2,0:T(8,128)}) %all-gather.9.cloned.1.call-update) | async-done | bytes 4194320 | tf_op jit(solution)/shard_map/all_gather | solution.py:46
  344.3 9.4 %bitcast_subtract_fusion = f32[1024,768]{0,1:T(8,128)S(1)} fusion(f32[768,1024]{1,0:T(8,128)} %fusion, f32[1024,768]{0,1:T(8,128)} %copy.22, f32[1024,768]{1,0:T(8,128)S(1)} %copy-done, f32[128,8,8,128]{3,2,1,0:T(8,128)} %bitcast.69), kind=kOutput, calls=%fused_computation.7 | convolution fusion | flops 4833411072 | bytes 16777216 | tf_op jit(solution)/shard_map/dot_general | solution.py:12
  353.8 2.6 pad_maximum_fusion
  356.4 6.0 %copy.18 = f32[1536,768]{1,0:T(8,128)} copy(f32[1536,768]{0,1:T(8,128)} %pad_maximum_fusion) | data formatting | bytes 9437184 | tf_op jit(solution)/shard_map/concatenate | solution.py:57
  (21 shorter events, 2.0 us)
Async XLA Ops:
  6.5 34.3 %all-gather.5.cloned.1.call-start = ((), (), s32[]{:S(2)}) async-start(), calls=%async_computation | async-start | bytes 2359296 | tf_op jit(solution)/shard_map/all_gather | solution.py:30
  7.3 56.9 %all-gather.7.cloned.1.call-start = ((), (), s32[]{:S(2)}) async-start(), calls=%async_computation.2 | async-start | bytes 1179648 | tf_op jit(solution)/shard_map/all_gather | solution.py:39
  8.9 144.9 %all-reduce.3.cloned.1.call-start = ((), (), s32[]{:S(2)}) async-start(), calls=%async_computation.1 | async-start | bytes 6291456 | tf_op jit(solution)/shard_map/psum | solution.py:38
  51.8 197.0 %all-reduce.5.cloned.1.call-start = ((), (), s32[]{:S(2)}) async-start(), calls=%async_computation.3 | async-start | bytes 6291456 | tf_op jit(solution)/shard_map/psum | solution.py:42
  158.6 4.0 %copy-start.3 = (f32[128,10,1,128]{3,2,1,0:T(1,128)S(1)}, f32[128,10,1,128]{3,2,1,0:T(1,128)}, u32[]{:S(2)}) copy-start(f32[128,10,1,128]{3,2,1,0:T(1,128)} %param.5) | copy-start | bytes 1966084
  161.7 135.4 %all-gather.11.cloned.1.call-start = ((), (), s32[]{:S(2)}) async-start(), calls=%async_computation.5 | async-start | bytes 4718592 | tf_op jit(solution)/shard_map/all_gather | solution.py:47
  162.3 182.0 %all-gather.9.cloned.1.call-start = ((), (), s32[]{:S(2)}) async-start(), calls=%async_computation.4 | async-start | bytes 4718592 | tf_op jit(solution)/shard_map/all_gather | solution.py:46
  167.2 4.1 %copy-start = (f32[1024,768]{1,0:T(8,128)S(1)}, f32[1024,768]{1,0:T(8,128)}, u32[]{:S(2)}) copy-start(f32[1024,768]{1,0:T(8,128)} %all-reduce.3.cloned.1.call-done) | copy-start | bytes 9437188
  344.3 9.4 %copy-start.1 = (f32[256,768]{0,1:T(8,128)S(1)}, f32[256,768]{0,1:T(8,128)}, u32[]{:S(2)}) copy-start(f32[256,768]{0,1:T(8,128)} %copy.20) | copy-start | bytes 2359300
  344.3 9.4 %copy-start.2 = (f32[96,8,2,128]{3,1,2,0:T(8,128)S(1)}, f32[96,8,2,128]{3,1,2,0:T(8,128)}, u32[]{:S(2)}) copy-start(f32[96,8,2,128]{3,1,2,0:T(8,128)} %copy.54) | copy-start | bytes 2359300
Sparse Core Ops, SparseCore 0:
  8.9 31.8 all-gather.4
  42.4 21.6 all-gather.6
  67.2 86.5 all-reduce.2
  161.9 86.9 all-reduce.4
  250.3 46.8 all-gather.10
  298.6 45.6 all-gather.8

commit v2 on v1

v2 whole, which is shorter than its diff:
```python
import functools

import jax
import jax.numpy as jnp
from jax import lax
from jax.experimental import pallas as pl
from jax.experimental.pallas import tpu as pltpu
from jax.sharding import PartitionSpec as P

MESH = pl.DeviceIdType.MESH
F32 = jnp.float32
BF16 = jnp.bfloat16


def split(value):
    high = value.astype(BF16)
    return high, (value - high.astype(F32)).astype(BF16)


def dot3(ah, al, bh, bl):
    d = functools.partial(jnp.dot, preferred_element_type=F32)
    return d(ah, bh) + (d(ah, bl) + d(al, bh))


def kernel(
    dims, k_ref, f_ref, s_ref, d_ref, out_ref,
    kg, ug, fg, sg, dg, kloc, bh, bl, dh, dl, wh, wl, wf, sems, osem,
):
    nrow, ncol, pc, rblk, kb, sem_count = dims
    nchip = ncol // 2
    nb = kb * ncol
    width = k_ref.shape[2]
    cycles = k_ref.shape[0]
    height = pc * rblk
    half_ring = nrow // 2
    row, col = lax.axis_index("row"), lax.axis_index("col")
    q, core = col // 2, col % 2
    partner = col + 1 - 2 * core

    def flip(i):
        return i + (i // half_ring) * (3 * half_ring - 1 - 2 * i)

    pos = flip(row)

    def row_at(shift):
        return flip((pos + shift + nrow) % nrow)

    table = {}

    def sem(*key):
        index = table.setdefault(key, len(table))
        assert index < sem_count
        return sems.at[index]

    sent = []

    def always(fn):
        fn()

    def guard(cond):
        return always if cond is None else pl.when(cond)

    def both(a, b):
        if a is None:
            return b
        return a if b is None else jnp.logical_and(a, b)

    def push(src, dst, skey, rkey, device, cond=None):
        copy = pltpu.make_async_remote_copy(
            src_ref=src, dst_ref=dst, send_sem=sem("s", *skey), recv_sem=sem("r", *rkey),
            device_id=device, device_id_type=MESH,
        )
        guard(cond)(copy.start)
        sent.append((cond, copy))

    def arrived(dst, rkey, device):
        pltpu.make_async_remote_copy(
            src_ref=dst, dst_ref=dst, send_sem=sem("s", *rkey), recv_sem=sem("r", *rkey),
            device_id=device, device_id_type=MESH,
        ).wait_recv()

    barrier = pltpu.get_barrier_semaphore()
    right, left = {"row": row_at(1)}, {"row": row_at(-1)}
    up, down, mate = {"col": col + 2}, {"col": col - 2}, {"col": partner}
    for device in (right, left, mate):
        pl.semaphore_signal(barrier, inc=1, device_id=device, device_id_type=MESH)
    has_up, has_down = q < nchip - 1, q > 0

    @pl.when(has_up)
    def _():
        pl.semaphore_signal(barrier, inc=1, device_id=up, device_id_type=MESH)

    @pl.when(has_down)
    def _():
        pl.semaphore_signal(barrier, inc=1, device_id=down, device_id_type=MESH)

    spans = nchip - 1
    pl.semaphore_wait(barrier, 3 + (2 * spans - 1 - q) // spans + (q + spans - 1) // spans)

    def fslot(lo, hi):
        return lambda chip, e: fg.at[pl.ds(pl.multiple_of((chip * 2 + e) * kb, kb), kb), lo:hi]

    def sslot(chip, e):
        return sg.at[pl.ds(pl.multiple_of((chip * 2 + e) * kb, kb), kb), :]

    def dslot(m, p):
        return lambda chip, e: dg.at[m, p, row, chip, e]

    low = [p * nchip // pc for p in range(pc)]
    chains = {}
    for m in range(2):
        for p in range(pc):
            chains["d", m, p] = (low[p], d_ref.at[m, p], dslot(m, p))
    chains["f1"] = (0, f_ref.at[:, :height], fslot(0, height))
    chains["f2"] = (0, f_ref.at[:, height:], fslot(height, f_ref.shape[1]))
    chains["s"] = (0, s_ref, sslot)

    def chain_own(name):
        first, src, slot = chains[name]
        mine = None if first == 0 else q >= first
        local = pltpu.make_async_copy(src, slot(q, core), sem("l", name))
        local.start()
        dst = slot(q, core)
        push(src, dst, (name, "u", 0), (name, "u", 1), up, both(mine, has_up))
        push(src, dst, (name, "d", 0), (name, "d", 1), down, both(mine, has_down))
        push(src, dst, (name, "m", 0), (name, "m", 0), mate, mine)
        return local

    def chain_hop(name, t):
        first, _, slot = chains[name]
        for way, source, more, nxt in (
            ("u", q - t, has_up, up), ("d", q + t, has_down, down)
        ):
            real = source >= first if way == "u" else source < nchip
            if way == "d" and first > 0:
                real = jnp.logical_and(real, source >= first)
            ref = slot(source, core)
            guard(real)(functools.partial(arrived, ref, (name, way, t), nxt))
            if t < nchip - 1:
                push(ref, ref, (name, way, t), (name, way, t + 1), nxt, both(real, more))
            push(ref, ref, (name, "m", way, t), (name, "m", way, t), mate, real)

    def chain_mate(name):
        first, _, slot = chains[name]
        other = 1 - core
        mine = None if first == 0 else q >= first
        guard(mine)(functools.partial(arrived, slot(q, other), (name, "m", 0), mate))
        for t in range(1, nchip):
            for way, source in (("u", q - t), ("d", q + t)):
                real = source >= first if way == "u" else source < nchip
                if way == "d" and first > 0:
                    real = jnp.logical_and(real, source >= first)
                guard(real)(
                    functools.partial(arrived, slot(source, other), (name, "m", way, t), mate)
                )

    def stack(buf):
        def place(origin, part, e):
            if part is None:
                return buf.at[:, origin]
            return buf.at[:, origin, pl.ds(part * (rblk // 2), rblk // 2), :]
        return place

    def dstack(m, p):
        def place(origin, part, e):
            if part is None:
                return dg.at[m, p, origin, low[p]:, e]
            return dg.at[m, p, origin, low[p]:, e, pl.ds(part * (kb // 2), kb // 2), :]
        return place

    rings = {"k": (stack(kg), False), "u": (stack(ug), False)}
    for m in range(2):
        for p in range(pc):
            rings["e", m, p] = (dstack(m, p), True)

    def ring_own(name, src=None):
        place, _ = rings[name]
        own = place(row, None, core)
        src = own if src is None else src
        push(src, own, (name, "R", 0), (name, "R", 1), right)
        push(src, own, (name, "L", 0), (name, "L", 1), left)

    def ring_hop(name, t):
        place, shared = rings[name]
        for way, sign, part, nxt in (("R", -1, 0, right), ("L", 1, 1, left)):
            origin = row_at(sign * t)
            got = None if t < half_ring else part
            ref = place(origin, got, core)
            arrived(ref, (name, way, t), nxt)
            if t < half_ring:
                fwd = place(origin, None if t + 1 < half_ring else part, core)
                push(fwd, fwd, (name, way, t), (name, way, t + 1), nxt)
            if shared:
                push(ref, ref, (name, "m", way, t), (name, "m", way, t), mate)

    def ring_mate(name):
        place, _ = rings[name]
        for t in range(1, half_ring + 1):
            for way, sign, part in (("R", -1, 0), ("L", 1, 1)):
                got = None if t < half_ring else part
                arrived(place(row_at(sign * t), got, 1 - core), (name, "m", way, t), mate)

    hops = range(1, nchip)
    rhops = range(1, half_ring + 1)
    dnames = [[("d", m, p) for p in range(pc)] for m in range(2)]
    enames = [[("e", m, p) for p in range(pc)] for m in range(2)]

    locals_ = {}
    for name in dnames[0] + ["f1"] + dnames[1]:
        locals_[name] = chain_own(name)
    ring_own("k", k_ref.at[:pc])
    kmine = pltpu.make_async_copy(k_ref.at[:pc], kg.at[:, row], sem("l", "k"))
    kmine.start()
    kall = pltpu.make_async_copy(k_ref.at[pc:], kloc, sem("l", "kall"))
    kall.start()
    for t in hops:
        for name in dnames[0]:
            chain_hop(name, t)
    for name, ring in zip(dnames[0], enames[0]):
        locals_[name].wait()
        ring_own(ring)
    for t in hops:
        chain_hop("f1", t)
    for t in hops:
        for name in dnames[1]:
            chain_hop(name, t)
    for name, ring in zip(dnames[1], enames[1]):
        locals_[name].wait()
    locals_["f2"] = chain_own("f2")
    locals_["s"] = chain_own("s")
    for t in rhops:
        ring_hop("k", t)
    for t in rhops:
        for ring in enames[0]:
            ring_hop(ring, t)
    for ring in enames[1]:
        ring_own(ring)
    for name in dnames[0]:
        chain_mate(name)
    for ring in enames[0]:
        ring_mate(ring)
    kmine.wait()

    group = nb // pc
    chunk = 256

    def solve(m, rhs, wbase):
        for p in range(pc):
            for r in range(nrow):
                at = (p * nrow + r) * rblk
                hi, lo = split(rhs[p, r])
                bh[at : at + rblk, :] = hi
                bl[at : at + rblk, :] = lo
                hi, lo = split(dg[m, p, r, low[p]:].reshape(nb - p * group, rblk))
                dh[p * group :, at : at + rblk] = hi
                dl[p * group :, at : at + rblk] = lo
        for g in range(pc):
            rows = slice(g * group, (g + 1) * group)
            deep = (g + 1) * group
            for n in range(0, width, chunk):
                cols = slice(n, n + chunk)
                w = dot3(dh[rows, :deep], dl[rows, :deep], bh[:deep, cols], bl[:deep, cols])
                wf[m, rows, cols] = w
                hi, lo = split(w)
                wh[m, rows, cols] = hi
                wl[m, rows, cols] = lo

    def apply(panel, lo, size, m):
        th, tl = split(panel[:, pl.ds(lo, size)].T)
        return dot3(th, tl, wh[m], wl[m])

    outs = []

    solve(0, kg, 0)
    chain_hop("f2", 1)
    locals_["f1"].wait()
    chain_mate("f1")
    kall.wait()
    first = apply(fg, 0, height, 0)
    ug[:, row] = kloc[:pc] - first.reshape(pc, rblk, width)
    ring_own("u")
    for p in range(pc):
        at = pl.multiple_of((p * nrow + row) * rblk, rblk)
        copy = pltpu.make_async_copy(wf.at[0, pl.ds(at, rblk), :], out_ref.at[p], osem.at[p])
        copy.start()
        outs.append(copy)
    for t in rhops:
        for ring in enames[1]:
            ring_hop(ring, t)
    chain_hop("s", 1)
    if nchip > 2:
        chain_hop("f2", 2)
    ring_hop("u", 1)
    if nchip > 2:
        chain_hop("s", 2)
    for t in rhops[1:]:
        ring_hop("u", t)
    for name in dnames[1]:
        chain_mate(name)
    for ring in enames[1]:
        ring_mate(ring)
    solve(1, ug, 0)
    for p in range(pc):
        at = pl.multiple_of((p * nrow + row) * rblk, rblk)
        copy = pltpu.make_async_copy(wf.at[1, pl.ds(at, rblk), :], out_ref.at[pc + p], osem.at[pc + p])
        copy.start()
        outs.append(copy)
    for t in range(3, nchip):
        chain_hop("f2", t)
    locals_["f2"].wait()
    chain_mate("f2")
    rest = cycles - 2 * pc
    tile = 2 if rest % 2 == 0 else 1
    size = tile * rblk

    def first_tile(i, carry):
        part = apply(fg, pl.multiple_of(height + i * size, rblk), size, 0)
        kloc[pl.ds(pc + i * tile, tile)] -= part.reshape(tile, rblk, width)
        return carry

    lax.fori_loop(0, rest // tile, first_tile, 0)
    for t in range(3, nchip):
        chain_hop("s", t)
    locals_["s"].wait()
    chain_mate("s")

    def second_tile(i, carry):
        part = apply(sg, pl.multiple_of(i * size, rblk), size, 1)
        kloc[pl.ds(pc + i * tile, tile)] -= part.reshape(tile, rblk, width)
        return carry

    lax.fori_loop(0, rest // tile, second_tile, 0)
    last = pltpu.make_async_copy(kloc.at[pc:], out_ref.at[2 * pc :], osem.at[2 * pc])
    last.start()
    outs.append(last)
    for cond, copy in sent:
        guard(cond)(copy.wait_send)
    for copy in outs:
        copy.wait()


def shards(stiffness, lower_first, lower_second, diag_inv):
    cycles, _, rblk, width = stiffness.shape
    nrow, ncol = lax.axis_size("row"), lax.axis_size("col")
    kb = lower_first.shape[0]
    pc = diag_inv.shape[2]
    nb = kb * ncol
    nchip = ncol // 2
    sem_count = (3 + 2 * pc) * (8 * nchip + 8) + 40 * (2 + 2 * pc) * max(1, nrow // 4)
    sem_count = 2 * sem_count
    dims = (nrow, ncol, pc, rblk, kb, sem_count)
    blocks = jnp.transpose(diag_inv[:, :, :, 0, :], (0, 2, 1, 3))
    out = pl.pallas_call(
        functools.partial(kernel, dims),
        out_shape=jax.ShapeDtypeStruct((cycles, rblk, width), F32),
        in_specs=[pl.BlockSpec(memory_space=pl.ANY)] * 4,
        out_specs=pl.BlockSpec(memory_space=pl.ANY),
        scratch_shapes=[
            pltpu.VMEM((pc, nrow, rblk, width), F32),
            pltpu.VMEM((pc, nrow, rblk, width), F32),
            pltpu.VMEM((nb, lower_first.shape[1] * rblk), F32),
            pltpu.VMEM((nb, lower_second.shape[1] * rblk), F32),
            pltpu.VMEM((2, pc, nrow, nchip, 2, kb, rblk), F32),
            pltpu.VMEM((cycles - pc, rblk, width), F32),
            pltpu.VMEM((nb, width), BF16),
            pltpu.VMEM((nb, width), BF16),
            pltpu.VMEM((nb, nb), BF16),
            pltpu.VMEM((nb, nb), BF16),
            pltpu.VMEM((2, nb, width), BF16),
            pltpu.VMEM((2, nb, width), BF16),
            pltpu.VMEM((2, nb, width), F32),
            pltpu.SemaphoreType.DMA((sem_count,)),
            pltpu.SemaphoreType.DMA((2 * pc + 1,)),
        ],
        compiler_params=pltpu.CompilerParams(
            collective_id=0, has_side_effects=True, vmem_limit_bytes=63 << 20
        ),
    )(
        stiffness.reshape(cycles, rblk, width),
        lower_first.reshape(kb, -1),
        lower_second.reshape(kb, -1),
        blocks,
    )
    return out.reshape(cycles, 1, rblk, width)


def solution(mesh):
    placed = (
        P(None, "row", None, "col"),
        P("col", None, "row", None),
        P("col", None, "row", None),
        P(None, "col", None, "row", None),
    )
    return jax.shard_map(
        shards, mesh=mesh, in_specs=placed, out_specs=P(None, "row", None, "col"), check_vma=False
    )
```

time: 370 us -> 141 us (0.38)
  waiting for transfers between devices: 283 us -> 0 us
  Pallas kernels: 0 us -> 129 us
  local copies, waits for them, and re-layouts: 39.8 us -> 9.51 us
  matrix products: 30 us -> 0 us
  between operations: 13.6 us -> 0.01 us
    psum x2 -> x0, waiting for transfers between devices: 164 us -> none  [the longest x1 89.7 us: shards(): w_first = lax.psum(product(inverse[0], matrix_rows[:height]), 'row')]
    pallas_call x0 -> x1, Pallas kernels: none -> 129 us  [shards(): pl.pallas_call(functools.partial(kernel, dims), out_shape=jax.ShapeDtypeS...]
    all_gather x4 -> x0, waiting for transfers between devices: 118 us -> none  [the longest x1 37.7 us: shards(): lax.all_gather(lower_second, 'col', axis=0, tiled=True)]
    dot_general x5 -> x0, matrix products: 30 us -> none  [the longest x3 23.8 us: apply_cols(): lax.dot_general(columns, factor, (((0,), (0,)), ((), ())), precision=lax....]
    slice x7 -> x0, local copies, waits for them, and re-layouts: 19.9 us -> none  [the longest x2 7.89 us: shards(): matrix_rows[2 * height:] - apply_cols(first_piece, w_first)]
    unnamed x9 -> x4, local copies, waits for them, and re-layouts: 0.97 us -> 9.51 us
    reshape x2 -> x0, local copies, waits for them, and re-layouts: 7.4 us -> none  [the longest x1 5.13 us: own_rows(): grouped = solved.reshape(pcount, nrow, rblk, cdev)]
    concatenate x1 -> x0, local copies, waits for them, and re-layouts: 6.04 us -> none  [shards(): jnp.concatenate([own_rows(w_first), own_rows(w_second), remain], axis=0)]
  transfers between devices with their start and end apart: 6 -> 0, of which waited for: 6 -> 0; matrix products, arithmetic and copies ran while one was open for 13% -> 0% of each run, Pallas kernels for 0% -> 0%
where the time goes in v2:
time: 141 us
  Pallas kernels  129 us (91%)
  local copies, waits for them, and re-layouts  9.51 us (7%)
  other arithmetic  2.67 us (2%)
    pallas_call x1, Pallas kernels, shards(): pl.pallas_call(functools.partial(kernel, dims), out_shape=jax.ShapeDtypeS...  129 us
    unnamed x4, local copies, waits for them, and re-layouts  9.51 us

profile of v2, /device:TPU:0, one launch (start us, length us, event | category | flops | bytes accessed | tf_op | source)
XLA Modules:
  0.0 140.8 jit_solution(7368327697668539535)
XLA Ops:
  0.0 1.7 %copy.14 = f32[2,128,2,1,128]{4,1,2,0,3:T(8,128)} copy(f32[2,128,2,1,128]{4,3,2,1,0:T(1,128)} %param.7) | data formatting | bytes 524288 | tf_op args[3]
  1.7 2.0 %copy.13 = f32[16,8,8,128]{3,1,2,0:T(8,128)} copy(f32[16,8,8,128]{3,2,1,0:T(8,128)} %bitcast.25) | data formatting | bytes 1048576
  3.6 2.7 %reduce = f32[128,10,128]{2,1,0:T(8,128)S(1)} reduce(f32[128,10,1,128]{3,2,1,0:T(1,128)} %param.5, f32[]{:T(128)} %constant.4), dimensions={2}, to_apply=%param.5.reduce_sub_computation | reduce | bytes 1310724 | tf_op args[1]
  6.3 1.1 copy.12
  7.4 128.6 %shard_map.46 = f32[12,128,768]{2,1,0:T(8,128)} custom-call(f32[12,128,768]{2,1,0:T(8,128)} %bitcast.20, f32[128,1280]{1,0:T(8,128)} %bitcast.22, f32[128,1024]{1,0:T(8,128)} %bitcast.23, f32[2,2,128,128]{3,2,1,0:T(8,128)} %bitcast.24), custom_call_target="tpu_custom_call" | custom-call | tf_op jit(solution)/shard_map/pallas_call | solution.py:353
  136.0 4.8 %copy.16 = f32[12,1,128,768]{3,2,1,0:T(8,128)} copy(f32[12,1,128,768]{3,2,1,0:T(8,128)} %bitcast.19) | data formatting | bytes 9437184

commit v3 on v2

--- a/solution.py
+++ b/solution.py
@@ -97,37 +97,53 @@
     spans = nchip - 1
     pl.semaphore_wait(barrier, 3 + (2 * spans - 1 - q) // spans + (q + spans - 1) // spans)
 
-    def fslot(lo, hi):
-        return lambda chip, e: fg.at[pl.ds(pl.multiple_of((chip * 2 + e) * kb, kb), kb), lo:hi]
-
-    def sslot(chip, e):
-        return sg.at[pl.ds(pl.multiple_of((chip * 2 + e) * kb, kb), kb), :]
+    def fslot(buf, lo, hi):
+        return lambda chip, e: buf.at[pl.ds(pl.multiple_of((chip * 2 + e) * kb, kb), kb), lo:hi]
 
     def dslot(m, p):
         return lambda chip, e: dg.at[m, p, row, chip, e]
 
     low = [p * nchip // pc for p in range(pc)]
+    rest = cycles - 2 * pc
+    cut = rest // 2 * rblk
     chains = {}
     for m in range(2):
         for p in range(pc):
-            chains["d", m, p] = (low[p], d_ref.at[m, p], dslot(m, p))
-    chains["f1"] = (0, f_ref.at[:, :height], fslot(0, height))
-    chains["f2"] = (0, f_ref.at[:, height:], fslot(height, f_ref.shape[1]))
-    chains["s"] = (0, s_ref, sslot)
-
-    def chain_own(name):
-        first, src, slot = chains[name]
+            chains["d", m, p] = (low[p], dslot(m, p), d_ref, None)
+    chains["f1"] = (0, fslot(fg, 0, height), f_ref, (0, pc))
+    chains["f2"] = (0, fslot(fg, height, height + rest * rblk), f_ref, (pc, pc + rest))
+    chains["s0"] = (0, fslot(sg, 0, cut), s_ref, (0, rest // 2))
+    chains["s1"] = (0, fslot(sg, cut, rest * rblk), s_ref, (rest // 2, rest))
+
+    def stage(name):
+        _, slot, src, span = chains[name]
+        if span is None:
+            _, m, p = name
+            pieces = [(src.at[m, :, p, 0, :], slot(q, core))]
+        else:
+            mine = slot(q, core)
+            pieces = [
+                (src.at[:, j, 0, :], mine.at[:, (j - span[0]) * rblk : (j - span[0] + 1) * rblk])
+                for j in range(*span)
+            ]
+        copies = []
+        for i, (here, there) in enumerate(pieces):
+            copies.append(pltpu.make_async_copy(here, there, sem("l", name, i)))
+            copies[-1].start()
+        return copies
+
+    def chain_own(name, copies):
+        first, slot, _, _ = chains[name]
+        for copy in copies:
+            copy.wait()
         mine = None if first == 0 else q >= first
-        local = pltpu.make_async_copy(src, slot(q, core), sem("l", name))
-        local.start()
-        dst = slot(q, core)
-        push(src, dst, (name, "u", 0), (name, "u", 1), up, both(mine, has_up))
-        push(src, dst, (name, "d", 0), (name, "d", 1), down, both(mine, has_down))
-        push(src, dst, (name, "m", 0), (name, "m", 0), mate, mine)
-        return local
+        own = slot(q, core)
+        push(own, own, (name, "u", 0), (name, "u", 1), up, both(mine, has_up))
+        push(own, own, (name, "d", 0), (name, "d", 1), down, both(mine, has_down))
+        push(own, own, (name, "m", 0), (name, "m", 0), mate, mine)
 
     def chain_hop(name, t):
-        first, _, slot = chains[name]
+        first, slot, _, _ = chains[name]
         for way, source, more, nxt in (
             ("u", q - t, has_up, up), ("d", q + t, has_down, down)
         ):
@@ -140,19 +156,19 @@
                 push(ref, ref, (name, way, t), (name, way, t + 1), nxt, both(real, more))
             push(ref, ref, (name, "m", way, t), (name, "m", way, t), mate, real)
 
-    def chain_mate(name):
-        first, _, slot = chains[name]
-        other = 1 - core
-        mine = None if first == 0 else q >= first
-        guard(mine)(functools.partial(arrived, slot(q, other), (name, "m", 0), mate))
-        for t in range(1, nchip):
-            for way, source in (("u", q - t), ("d", q + t)):
-                real = source >= first if way == "u" else source < nchip
-                if way == "d" and first > 0:
-                    real = jnp.logical_and(real, source >= first)
-                guard(real)(
-                    functools.partial(arrived, slot(source, other), (name, "m", way, t), mate)
-                )
+    def chain_mate(name, t):
+        first, slot, _, _ = chains[name]
+        if t == 0:
+            mine = None if first == 0 else q >= first
+            guard(mine)(functools.partial(arrived, slot(q, 1 - core), (name, "m", 0), mate))
+            return
+        for way, source in (("u", q - t), ("d", q + t)):
+            real = source >= first if way == "u" else source < nchip
+            if way == "d" and first > 0:
+                real = jnp.logical_and(real, source >= first)
+            guard(real)(
+                functools.partial(arrived, slot(source, 1 - core), (name, "m", way, t), mate)
+            )
 
     def stack(buf):
         def place(origin, part, e):
@@ -205,55 +221,26 @@
     dnames = [[("d", m, p) for p in range(pc)] for m in range(2)]
     enames = [[("e", m, p) for p in range(pc)] for m in range(2)]
 
-    locals_ = {}
-    for name in dnames[0] + ["f1"] + dnames[1]:
-        locals_[name] = chain_own(name)
-    ring_own("k", k_ref.at[:pc])
-    kmine = pltpu.make_async_copy(k_ref.at[:pc], kg.at[:, row], sem("l", "k"))
-    kmine.start()
-    kall = pltpu.make_async_copy(k_ref.at[pc:], kloc, sem("l", "kall"))
-    kall.start()
-    for t in hops:
-        for name in dnames[0]:
-            chain_hop(name, t)
-    for name, ring in zip(dnames[0], enames[0]):
-        locals_[name].wait()
-        ring_own(ring)
-    for t in hops:
-        chain_hop("f1", t)
-    for t in hops:
-        for name in dnames[1]:
-            chain_hop(name, t)
-    for name, ring in zip(dnames[1], enames[1]):
-        locals_[name].wait()
-    locals_["f2"] = chain_own("f2")
-    locals_["s"] = chain_own("s")
-    for t in rhops:
-        ring_hop("k", t)
-    for t in rhops:
-        for ring in enames[0]:
-            ring_hop(ring, t)
-    for ring in enames[1]:
-        ring_own(ring)
-    for name in dnames[0]:
-        chain_mate(name)
-    for ring in enames[0]:
-        ring_mate(ring)
-    kmine.wait()
-
     group = nb // pc
     chunk = 256
 
-    def solve(m, rhs, wbase):
+    def right_side(rhs):
         for p in range(pc):
             for r in range(nrow):
                 at = (p * nrow + r) * rblk
                 hi, lo = split(rhs[p, r])
                 bh[at : at + rblk, :] = hi
                 bl[at : at + rblk, :] = lo
+
+    def left_side(m):
+        for p in range(pc):
+            for r in range(nrow):
+                at = (p * nrow + r) * rblk
                 hi, lo = split(dg[m, p, r, low[p]:].reshape(nb - p * group, rblk))
                 dh[p * group :, at : at + rblk] = hi
                 dl[p * group :, at : at + rblk] = lo
+
+    def solve(m):
         for g in range(pc):
             rows = slice(g * group, (g + 1) * group)
             deep = (g + 1) * group
@@ -265,74 +252,137 @@
                 wh[m, rows, cols] = hi
                 wl[m, rows, cols] = lo
 
-    def apply(panel, lo, size, m):
-        th, tl = split(panel[:, pl.ds(lo, size)].T)
-        return dot3(th, tl, wh[m], wl[m])
-
     outs = []
 
-    solve(0, kg, 0)
-    chain_hop("f2", 1)
-    locals_["f1"].wait()
-    chain_mate("f1")
+    def emit(src, dst, index):
+        copy = pltpu.make_async_copy(src, dst, osem.at[index])
+        copy.start()
+        outs.append(copy)
+
+    def own_rows(m):
+        for p in range(pc):
+            at = pl.multiple_of((p * nrow + row) * rblk, rblk)
+            emit(wf.at[m, pl.ds(at, rblk), :], out_ref.at[m * pc + p], m * pc + p)
+
+    deep = 2 * kb
+
+    def slab(panel, begin, block, count, m, chip):
+        tile = 2 if count % 2 == 0 else 1
+        size = tile * rblk
+        rows = pl.ds(pl.multiple_of(chip * deep, deep), deep)
+
+        def step(i, carry):
+            cols = pl.ds(pl.multiple_of(begin + i * size, rblk), size)
+            th, tl = split(panel[rows, cols].T)
+            part = dot3(th, tl, wh[m, rows, :], wl[m, rows, :])
+            kloc[pl.ds(block + i * tile, tile)] -= part.reshape(tile, rblk, width)
+            return carry
+
+        lax.fori_loop(0, count // tile, step, 0)
+
+    first_half, second_half = rest // 2, rest - rest // 2
+    uses = {
+        "f2": (fg, height, pc, rest, 0),
+        "s0": (sg, 0, pc, first_half, 1),
+        "s1": (sg, cut, pc + first_half, second_half, 1),
+    }
+
+    def phase(name, t):
+        chain_mate(name, t)
+        if t == 0:
+            slab(*uses[name], q)
+            return
+        for source, real in ((q - t, q >= t), (q + t, q + t < nchip)):
+            pl.when(real)(functools.partial(slab, *uses[name], source))
+
+    def hop(name, t):
+        if t < nchip:
+            chain_hop(name, t)
+
+    panels = ("s0", "s1")
+    ring_own("k", k_ref.at[:pc])
+    staged = {name: stage(name) for name in chains}
+    kmine = pltpu.make_async_copy(k_ref.at[:pc], kg.at[:, row], sem("l", "k"))
+    kmine.start()
+    kall = pltpu.make_async_copy(k_ref.at[pc:], kloc, sem("l", "kall"))
+    kall.start()
+    for name in dnames[0] + ["f1"] + dnames[1]:
+        chain_own(name, staged[name])
+    for t in hops:
+        for name in dnames[0]:
+            chain_hop(name, t)
+    for ring in enames[0]:
+        ring_own(ring)
+    for t in hops:
+        for name in ["f1"] + dnames[1]:
+            chain_hop(name, t)
+    for name in ("f2",) + panels:
+        chain_own(name, staged[name])
+    for t in rhops[:-1]:
+        ring_hop("k", t)
+    for ring in enames[1]:
+        ring_own(ring)
+    for t in rhops[:-1]:
+        for ring in enames[0]:
+            ring_hop(ring, t)
+    ring_hop("k", half_ring)
+    kmine.wait()
+    right_side(kg)
+    for ring in enames[0]:
+        ring_hop(ring, half_ring)
+    for t in range(nchip):
+        for name in dnames[0]:
+            chain_mate(name, t)
+    for ring in enames[0]:
+        ring_mate(ring)
+    left_side(0)
+    solve(0)
+    hop("f2", 1)
+    for t in range(nchip):
+        chain_mate("f1", t)
     kall.wait()
-    first = apply(fg, 0, height, 0)
+    th, tl = split(fg[:, :height].T)
+    first = dot3(th, tl, wh[0], wl[0])
     ug[:, row] = kloc[:pc] - first.reshape(pc, rblk, width)
     ring_own("u")
-    for p in range(pc):
-        at = pl.multiple_of((p * nrow + row) * rblk, rblk)
-        copy = pltpu.make_async_copy(wf.at[0, pl.ds(at, rblk), :], out_ref.at[p], osem.at[p])
-        copy.start()
-        outs.append(copy)
-    for t in rhops:
+    own_rows(0)
+    for t in rhops[:-1]:
         for ring in enames[1]:
             ring_hop(ring, t)
-    chain_hop("s", 1)
-    if nchip > 2:
-        chain_hop("f2", 2)
-    ring_hop("u", 1)
-    if nchip > 2:
-        chain_hop("s", 2)
-    for t in rhops[1:]:
-        ring_hop("u", t)
-    for name in dnames[1]:
-        chain_mate(name)
+    phase("f2", 0)
+    for name in panels:
+        hop(name, 1)
+    for ring in enames[1]:
+        ring_hop(ring, half_ring)
+    for t in range(nchip):
+        for name in dnames[1]:
+            chain_mate(name, t)
     for ring in enames[1]:
         ring_mate(ring)
-    solve(1, ug, 0)
-    for p in range(pc):
-        at = pl.multiple_of((p * nrow + row) * rblk, rblk)
-        copy = pltpu.make_async_copy(wf.at[1, pl.ds(at, rblk), :], out_ref.at[pc + p], osem.at[pc + p])
-        copy.start()
-        outs.append(copy)
+    left_side(1)
+    phase("f2", 1)
+    hop("f2", 2)
+    for t in rhops[:-1]:
+        ring_hop("u", t)
+    if nchip > 2:
+        phase("f2", 2)
+    for name in panels:
+        hop(name, 2)
+    ring_hop("u", half_ring)
+    right_side(ug)
+    solve(1)
+    own_rows(1)
+    for t in range(min(3, nchip)):
+        for name in panels:
+            phase(name, t)
     for t in range(3, nchip):
-        chain_hop("f2", t)
-    locals_["f2"].wait()
-    chain_mate("f2")
-    rest = cycles - 2 * pc
-    tile = 2 if rest % 2 == 0 else 1
-    size = tile * rblk
-
-    def first_tile(i, carry):
-        part = apply(fg, pl.multiple_of(height + i * size, rblk), size, 0)
-        kloc[pl.ds(pc + i * tile, tile)] -= part.reshape(tile, rblk, width)
-        return carry
-
-    lax.fori_loop(0, rest // tile, first_tile, 0)
-    for t in range(3, nchip):
-        chain_hop("s", t)
-    locals_["s"].wait()
-    chain_mate("s")
-
-    def second_tile(i, carry):
-        part = apply(sg, pl.multiple_of(i * size, rblk), size, 1)
-        kloc[pl.ds(pc + i * tile, tile)] -= part.reshape(tile, rblk, width)
-        return carry
-
-    lax.fori_loop(0, rest // tile, second_tile, 0)
-    last = pltpu.make_async_copy(kloc.at[pc:], out_ref.at[2 * pc :], osem.at[2 * pc])
-    last.start()
-    outs.append(last)
+        hop("f2", t)
+        phase("f2", t)
+        for name in panels:
+            hop(name, t)
+        for name in panels:
+            phase(name, t)
+    emit(kloc.at[pc:], out_ref.at[2 * pc :], 2 * pc)
     for cond, copy in sent:
         guard(cond)(copy.wait_send)
     for copy in outs:
@@ -346,10 +396,9 @@
     pc = diag_inv.shape[2]
     nb = kb * ncol
     nchip = ncol // 2
-    sem_count = (3 + 2 * pc) * (8 * nchip + 8) + 40 * (2 + 2 * pc) * max(1, nrow // 4)
-    sem_count = 2 * sem_count
+    sem_count = (4 + 2 * pc) * (8 * nchip + 8) + 40 * (2 + 2 * pc) * max(1, nrow // 4)
+    sem_count = 2 * sem_count + 2 * lower_first.shape[1]
     dims = (nrow, ncol, pc, rblk, kb, sem_count)
-    blocks = jnp.transpose(diag_inv[:, :, :, 0, :], (0, 2, 1, 3))
     out = pl.pallas_call(
         functools.partial(kernel, dims),
         out_shape=jax.ShapeDtypeStruct((cycles, rblk, width), F32),
@@ -377,9 +426,9 @@
         ),
     )(
         stiffness.reshape(cycles, rblk, width),
-        lower_first.reshape(kb, -1),
-        lower_second.reshape(kb, -1),
-        blocks,
+        lower_first,
+        lower_second,
+        diag_inv,
     )
     return out.reshape(cycles, 1, rblk, width)
 

time: 141 us -> 134 us (0.950)
  local copies, waits for them, and re-layouts: 9.51 us -> 4.83 us
  other arithmetic: 2.67 us -> 0 us
    unnamed x4 -> x1, local copies, waits for them, and re-layouts: 9.51 us -> 4.83 us
    unnamed x1 -> x0, other arithmetic: 2.67 us -> none
where the time goes in v3:
time: 134 us; the launch traced here: 133 us
  Pallas kernels  129 us (96%)
  local copies, waits for them, and re-layouts  4.83 us (4%)
    pallas_call x1, Pallas kernels, shards(): pl.pallas_call(functools.partial(kernel, dims), out_shape=jax.ShapeDtypeS...  129 us
    unnamed x1, local copies, waits for them, and re-layouts  4.83 us

profile of v3, /device:TPU:0, one launch (start us, length us, event | category | flops | bytes accessed | tf_op | source)
XLA Modules:
  0.0 133.4 jit_solution(17205999458471293536)
XLA Ops:
  0.0 128.6 %shard_map.46 = f32[12,128,768]{2,1,0:T(8,128)} custom-call(f32[12,128,768]{2,1,0:T(8,128)} %bitcast.5, f32[128,10,1,128]{3,2,1,0:T(1,128)} %f_ref.1, f32[128,8,1,128]{3,2,1,0:T(1,128)} %s_ref.1, f32[2,128,2,1,128]{4,3,2,1,0:T(1,128)} %d_ref.1), custom_call_target="tpu_custom_call" | custom-call | tf_op jit(solution)/shard_map/pallas_call | solution.py:402
  128.6 4.8 %copy.7 = f32[12,1,128,768]{3,2,1,0:T(8,128)} copy(f32[12,1,128,768]{3,2,1,0:T(8,128)} %bitcast.4) | data formatting | bytes 9437184

commit v4 on v3

--- a/solution.py
+++ b/solution.py
@@ -313,21 +313,26 @@
             chain_hop(name, t)
     for ring in enames[0]:
         ring_own(ring)
-    for t in hops:
-        for name in ["f1"] + dnames[1]:
+    early = ["f1"] + dnames[1]
+    for name in early:
+        chain_hop(name, 1)
+    chain_own("f2", staged["f2"])
+    for t in hops[1:]:
+        for name in early:
             chain_hop(name, t)
-    for name in ("f2",) + panels:
+    for name in panels:
         chain_own(name, staged[name])
     for t in rhops[:-1]:
         ring_hop("k", t)
-    for ring in enames[1]:
-        ring_own(ring)
     for t in rhops[:-1]:
         for ring in enames[0]:
             ring_hop(ring, t)
+    for ring in enames[1]:
+        ring_own(ring)
     ring_hop("k", half_ring)
     kmine.wait()
     right_side(kg)
+    hop("f2", 1)
     for ring in enames[0]:
         ring_hop(ring, half_ring)
     for t in range(nchip):
@@ -337,7 +342,6 @@
         ring_mate(ring)
     left_side(0)
     solve(0)
-    hop("f2", 1)
     for t in range(nchip):
         chain_mate("f1", t)
     kall.wait()
@@ -345,13 +349,13 @@
     first = dot3(th, tl, wh[0], wl[0])
     ug[:, row] = kloc[:pc] - first.reshape(pc, rblk, width)
     ring_own("u")
-    own_rows(0)
     for t in rhops[:-1]:
         for ring in enames[1]:
             ring_hop(ring, t)
-    phase("f2", 0)
     for name in panels:
         hop(name, 1)
+    own_rows(0)
+    phase("f2", 0)
     for ring in enames[1]:
         ring_hop(ring, half_ring)
     for t in range(nchip):
@@ -359,15 +363,15 @@
             chain_mate(name, t)
     for ring in enames[1]:
         ring_mate(ring)
+    hop("f2", 2)
     left_side(1)
     phase("f2", 1)
-    hop("f2", 2)
+    for name in panels:
+        hop(name, 2)
     for t in rhops[:-1]:
         ring_hop("u", t)
     if nchip > 2:
         phase("f2", 2)
-    for name in panels:
-        hop(name, 2)
     ring_hop("u", half_ring)
     right_side(ug)
     solve(1)

time: 134 us -> 141 us (1.052)
  Pallas kernels: 129 us -> 136 us
    pallas_call x1, Pallas kernels: 129 us -> 136 us  [shards(): pl.pallas_call(functools.partial(kernel, dims), out_shape=jax.ShapeDtypeS...]
where the time goes in v4:
time: 141 us; the launch traced here: 140 us
  Pallas kernels  136 us (96%)
  local copies, waits for them, and re-layouts  4.83 us (3%)
    pallas_call x1, Pallas kernels, shards(): pl.pallas_call(functools.partial(kernel, dims), out_shape=jax.ShapeDtypeS...  136 us
    unnamed x1, local copies, waits for them, and re-layouts  4.83 us

profile of v4, /device:TPU:0, one launch (start us, length us, event | category | flops | bytes accessed | tf_op | source)
XLA Modules:
  0.0 140.4 jit_solution(14498622668109645593)
XLA Ops:
  0.0 135.6 %shard_map.46 = f32[12,128,768]{2,1,0:T(8,128)} custom-call(f32[12,128,768]{2,1,0:T(8,128)} %bitcast.5, f32[128,10,1,128]{3,2,1,0:T(1,128)} %f_ref.1, f32[128,8,1,128]{3,2,1,0:T(1,128)} %s_ref.1, f32[2,128,2,1,128]{4,3,2,1,0:T(1,128)} %d_ref.1), custom_call_target="tpu_custom_call" | custom-call | tf_op jit(solution)/shard_map/pallas_call | solution.py:406
  135.6 4.8 %copy.7 = f32[12,1,128,768]{3,2,1,0:T(8,128)} copy(f32[12,1,128,768]{3,2,1,0:T(8,128)} %bitcast.4) | data formatting | bytes 9437184
